TPU v7x, 32 devices: a whole 2x2x4 slice. The times are simulated.
32 devices in a mesh: parts: 2 (over x), rows: 16 (over z, y, core).
Axes of the slice: x: 2, y: 2, z: 4, core: 2. Of those that a mesh axis runs over, the one named last changes fastest.
Arguments:
- rhs: float32 [3, 12288, 256], P(None, 'rows', 'parts'), parts along dimension 2, may hold values from -6 to 6
- diag_inv: float32 [3, 12288, 768], P(None, 'rows'), may hold values from -0.21875 to 0.21875
- tiles: float32 [2, 32, 768, 768], P(None, 'rows'), may hold values from -0.15625 to 0.15625
- dest: int32 [2, 16, 2], P(None, 'rows'), may hold values from 0 to 15, all different within a row; in each aligned block of 16 rows (0 to 15, 16 to 31, ..., all dimensions but the last counted through in order) at most 4 rows name the same one
- obs_weight: float32 [12288], P('rows'), may hold values from -0.108253175 to 0.108253175, as said below
Outputs:
- solution: float32 [3, 12288, 256], P(None, 'rows', 'parts'), parts along dimension 2
- observed: float32 [256], P('parts'), parts along dimension 0
There are 2 independent parts, one for each index of `parts`. A program takes and returns all parts, laid end to end along the dimension named above; an argument that names none is the same for every part. Nothing has to cross between parts.
Inputs may be any that keep to these rules, and one draw needn't show every extreme that they name: `dest`: in each of the two levels, the two entries of a supernode differ, and no supernode of the next level is named more than 4 times. `obs_weight`: finite weights.
All inputs are finite; a program needn't handle non-finite values.
Results may differ from a plain program's by a relative error of at most 0.00029.
Values sent between devices are 32-bit elements; how exact they have to be, the bound alone decides.
No kernel may reach another device: no remote copies, remote signals or barrier semaphores. Data moves between devices by JAX's collectives and lax.ppermute only.
A program may use at most 128 MiB of HBM per device.

v0:
```python
import jax
import jax.numpy as jnp
from jax import lax
from jax.sharding import PartitionSpec as P


def collect_updates(solved_block, tiles_level, pattern_level):
    products = jnp.einsum(
        "kab,bc->kac",
        tiles_level,
        solved_block,
        precision=lax.Precision.HIGHEST,
        preferred_element_type=jnp.float32,
    )
    block_rows = solved_block.shape[0]
    width = products.shape[2]
    count = lax.axis_size("rows")
    sliced = lax.all_to_all(products, "rows", split_axis=1, concat_axis=0, tiled=True)
    owners = jnp.arange(count, dtype=jnp.int32)
    flat_targets = pattern_level.reshape(-1)
    matches = (owners[:, None] == flat_targets[None, :]).astype(jnp.float32)
    partial_value = jnp.einsum("mq,qac->mac", matches, sliced, precision=lax.Precision.HIGHEST)
    returned = lax.all_to_all(partial_value, "rows", split_axis=0, concat_axis=0, tiled=True)
    return returned.reshape(block_rows, width)


def body(rhs, diag_inv, tiles, dest, obs_weight):
    pattern = lax.all_gather(dest, "rows", axis=1, tiled=True)
    current = rhs[0]
    solved_levels = []
    solved_block = current
    for section in range(3):
        solved_block = jnp.dot(
            diag_inv[section],
            current,
            precision=lax.Precision.HIGHEST,
            preferred_element_type=jnp.float32,
        )
        solved_levels.append(solved_block)
        if section < 2:
            current = rhs[section + 1] - collect_updates(
                solved_block, tiles[section], pattern[section]
            )
    partial_sum = jnp.dot(
        obs_weight,
        solved_block,
        precision=lax.Precision.HIGHEST,
        preferred_element_type=jnp.float32,
    )
    observed = lax.psum(partial_sum, "rows")
    return (jnp.stack(solved_levels), observed)


def solution(mesh):
    in_specs = (
        P(None, "rows", "parts"),
        P(None, "rows", None),
        P(None, "rows", None, None),
        P(None, "rows", None),
        P("rows"),
    )
    out_specs = (P(None, "rows", "parts"), P("parts"))
    return jax.shard_map(body, mesh=mesh, in_specs=in_specs, out_specs=out_specs, check_vma=False)
```

profile of v0, /device:TPU:0, one launch (start us, length us, event | category | flops | bytes accessed | tf_op | source)
XLA Modules:
  0.0 156.5 jit_solution(14306570408259959369)
XLA Ops:
  0.6 3.7 %fusion.10 = f32[768,128]{1,0:T(8,128)S(1)} fusion(f32[3,768,768]{2,1,0:T(8,128)} %param.6, f32[3,768,128]{2,1,0:T(8,128)} %param.5), kind=kOutput, calls=%fused_computation.10 | convolution fusion | flops 905969664 | bytes 3145728 | tf_op jit(solution)/shard_map/dot_general | solution.py:33
  4.3 7.4 %fusion.15 = f32[2,768,128]{1,2,0:T(8,128)S(1)} fusion(f32[2,2,768,768]{3,2,1,0:T(8,128)} %param.7, f32[768,128]{1,0:T(8,128)S(1)} %fusion.10), kind=kOutput, calls=%fused_computation.15 | convolution fusion | flops 1811939328 | bytes 5898240 | tf_op jit(solution)/shard_map/kab,bc->kac/dot_general | solution.py:8
  11.7 0.0 copy-start.3
  11.7 1.2 copy.23
  12.9 7.5 %all-to-all-start = ((f32[2,768,128]{2,0,1:T(2,128)}), f32[2,768,128]{2,0,1:T(2,128)S(1)}, u32[]{:S(2)}, u32[]{:S(2)}) async-start(f32[2,768,128]{2,0,1:T(2,128)} %copy.23), calls=%async_computation | async-start | bytes 1572864 | tf_op jit(solution)/shard_map/all_to_all | solution.py:18
  20.4 29.2 %all_gather.3 = s32[2,16,2]{2,0,1:T(2,128)S(1)} all-gather(s32[2,1,2]{2,0,1:T(2,128)S(1)} %bitcast.82), channel_id=1, replica_groups=mesh['parts'=2,'rows'=16] {'rows'}, dimensions={1}, use_global_device_ids=true | all-gather | bytes 272 | tf_op jit(solution)/shard_map/all_gather | solution.py:28
  49.7 0.1 eq.31
  49.8 0.0 copy-start
  49.8 0.1 copy.24
  49.8 0.6 copy.25
  50.5 0.4 fusion.29
  50.8 0.1 copy.26
  51.0 16.7 %all_to_all.46 = f32[16,48,128]{2,1,0:T(8,128)S(1)} all-to-all(f32[16,48,128]{2,1,0:T(8,128)S(1)} %copy.26), channel_id=1, replica_groups=mesh['parts'=2,'rows'=16] {'rows'}, dimensions={0} | all-to-all | bytes 786432 | tf_op jit(solution)/shard_map/all_to_all | solution.py:23
  67.7 0.1 bitcast_subtract_fusion.1
  67.8 3.8 %fusion.8 = f32[128,768]{1,0:T(8,128)S(1)} fusion(f32[3,768,768]{2,1,0:T(8,128)} %param.6, f32[1,768,128]{2,1,0:T(8,128)S(1)} %bitcast_subtract_fusion.1), kind=kOutput, calls=%fused_computation.8 | convolution fusion | flops 905969664 | bytes 3145728 | tf_op jit(solution)/shard_map/dot_general | solution.py:33
  71.5 5.0 %fusion.18 = f32[2,768,128]{1,2,0:T(8,128)S(1)} fusion(f32[2,2,768,768]{3,2,1,0:T(8,128)S(1)} %copy-done, f32[128,768]{1,0:T(8,128)S(1)} %fusion.8), kind=kOutput, calls=%fused_computation.16 | convolution fusion | flops 1811939328 | bytes 5898240 | tf_op jit(solution)/shard_map/kab,bc->kac/dot_general | solution.py:8
  76.5 1.2 copy.28
  77.7 3.6 %all-to-all-start.2 = ((f32[2,768,128]{2,0,1:T(2,128)}), f32[2,768,128]{2,0,1:T(2,128)S(1)}, u32[]{:S(2)}, u32[]{:S(2)}) async-start(f32[2,768,128]{2,0,1:T(2,128)} %copy.28), calls=%async_computation.2 | async-start | bytes 1572864 | tf_op jit(solution)/shard_map/all_to_all | solution.py:18
  81.3 0.1 eq.35
  81.4 18.6 %all-to-all-done.2 = f32[2,768,128]{2,0,1:T(2,128)S(1)} async-done(((f32[2,768,128]{2,0,1:T(2,128)}), f32[2,768,128]{2,0,1:T(2,128)S(1)}, u32[]{:S(2)}, u32[]{:S(2)}) %all-to-all-start.2) | async-done | bytes 786464 | tf_op jit(solution)/shard_map/all_to_all | solution.py:18
  99.9 0.1 copy.29
  100.0 0.0 copy-start.2
  100.0 0.6 copy.30
  100.6 0.4 fusion.32
  101.0 0.9 copy.31
  101.9 5.3 %all-to-all-start.3 = ((f32[16,48,128]{2,1,0:T(8,128)}), f32[16,48,128]{2,1,0:T(8,128)S(1)}, u32[]{:S(2)}, u32[]{:S(2)}) async-start(f32[16,48,128]{2,1,0:T(8,128)} %copy.31), calls=%async_computation.3 | async-start | bytes 786432 | tf_op jit(solution)/shard_map/all_to_all | solution.py:23
  107.3 0.2 copy.27
  107.4 12.0 %all-to-all-done.3 = f32[16,48,128]{2,1,0:T(8,128)S(1)} async-done(((f32[16,48,128]{2,1,0:T(8,128)}), f32[16,48,128]{2,1,0:T(8,128)S(1)}, u32[]{:S(2)}, u32[]{:S(2)}) %all-to-all-start.3) | async-done | bytes 393248 | tf_op jit(solution)/shard_map/all_to_all | solution.py:23
  119.4 3.7 %fusion.6 = f32[128,768]{0,1:T(8,128)S(1)} fusion(f32[3,768,768]{2,1,0:T(8,128)} %param.6, f32[1,768,128]{2,1,0:T(8,128)S(1)} %bitcast_subtract_fusion), kind=kOutput, calls=%fused_computation.6 | convolution fusion | flops 905969664 | bytes 3145728 | tf_op jit(solution)/shard_map/dot_general | solution.py:33
  123.1 0.3 convolution_bitcast_fusion
  123.4 32.0 %psum.7 = f32[128]{0:T(128)} all-reduce(f32[128]{0:T(128)S(1)} %convolution_bitcast_fusion), channel_id=1, replica_groups=mesh['parts'=2,'rows'=16] {'rows'}, use_global_device_ids=true, to_apply=%region_0.0 | all-reduce | flops 128 | bytes 1024 | tf_op jit(solution)/shard_map/psum | solution.py:50
  155.4 1.1 pad_maximum_fusion
  (9 shorter events, 0.1 us)
Async XLA Ops:
  11.7 8.7 %copy-start.3 = (s32[2,1,2]{2,1,0:T(1,128)S(1)}, s32[2,1,2]{2,1,0:T(1,128)}, u32[]{:S(2)}) copy-start(s32[2,1,2]{2,1,0:T(1,128)} %param.8) | copy-start | bytes 52
  12.9 54.8 %copy-start.1 = (f32[3,768,128]{2,1,0:T(8,128)S(1)}, f32[3,768,128]{2,1,0:T(8,128)}, u32[]{:S(2)}) copy-start(f32[3,768,128]{2,1,0:T(8,128)} %param.5) | copy-start | bytes 3538948
  12.9 36.9 %all-to-all-start = ((f32[2,768,128]{2,0,1:T(2,128)}), f32[2,768,128]{2,0,1:T(2,128)S(1)}, u32[]{:S(2)}, u32[]{:S(2)}) async-start(f32[2,768,128]{2,0,1:T(2,128)} %copy.23), calls=%async_computation | async-start | bytes 1572864 | tf_op jit(solution)/shard_map/all_to_all | solution.py:18
  49.8 21.8 %copy-start = (f32[2,2,768,768]{3,2,1,0:T(8,128)S(1)}, f32[2,2,768,768]{3,2,1,0:T(8,128)}, u32[]{:S(2)}) copy-start(f32[2,2,768,768]{3,2,1,0:T(8,128)} %param.7) | copy-start | bytes 28311556
  77.7 22.3 %all-to-all-start.2 = ((f32[2,768,128]{2,0,1:T(2,128)}), f32[2,768,128]{2,0,1:T(2,128)S(1)}, u32[]{:S(2)}, u32[]{:S(2)}) async-start(f32[2,768,128]{2,0,1:T(2,128)} %copy.28), calls=%async_computation.2 | async-start | bytes 1572864 | tf_op jit(solution)/shard_map/all_to_all | solution.py:18
  100.0 7.2 %copy-start.2 = (f32[768]{0:T(1024)S(1)}, f32[768]{0:T(1024)}, u32[]{:S(2)}) copy-start(f32[768]{0:T(1024)} %param.9) | copy-start | bytes 9220
  101.9 17.5 %all-to-all-start.3 = ((f32[16,48,128]{2,1,0:T(8,128)}), f32[16,48,128]{2,1,0:T(8,128)S(1)}, u32[]{:S(2)}, u32[]{:S(2)}) async-start(f32[16,48,128]{2,1,0:T(8,128)} %copy.31), calls=%async_computation.3 | async-start | bytes 786432 | tf_op jit(solution)/shard_map/all_to_all | solution.py:23
where the time goes:
time: 157 us
  blocking collectives  77.9 us (50%)
  waiting for transfers between devices  30.5 us (19%)
  matrix products  24.5 us (16%)
  starting transfers between devices  16.5 us (11%)
  local copies, waits for them, and re-layouts  5.05 us (3%)
    psum x1, blocking collectives, body(): observed = lax.psum(partial_sum, 'rows')  32 us
    all_gather x1, blocking collectives, body(): pattern = lax.all_gather(dest, 'rows', axis=1, tiled=True)  29.2 us
    all_to_all x2, waiting for transfers between devices, collect_updates(): lax.all_to_all(products, 'rows', split_axis=1, concat_axis=0, tiled=True)  18.6 us
    all_to_all x1, blocking collectives, collect_updates(): lax.all_to_all(partial_value, 'rows', split_axis=0, concat_axis=0, tiled=...  16.7 us
    dot_general x2, matrix products, collect_updates(): jnp.einsum('kab,bc->kac', tiles_level, solved_block, precision=lax.Precis...  12.3 us
    all_to_all x1, waiting for transfers between devices, collect_updates(): lax.all_to_all(partial_value, 'rows', split_axis=0, concat_axis=0, tiled=...  12 us
    all_to_all x2, starting transfers between devices, collect_updates(): lax.all_to_all(products, 'rows', split_axis=1, concat_axis=0, tiled=True)  11.2 us
    dot_general x3, matrix products, body(): jnp.dot(diag_inv[section], current, precision=lax.Precision.HIGHEST, pref...  11.1 us
  transfers between devices with their start and end apart: 3, of which 2 were waited for; matrix products, arithmetic and copies ran while one was open for 0% of the time, Pallas kernels for 0%

commit v1 on v0

--- a/solution.py
+++ b/solution.py
@@ -25,7 +25,7 @@
 
 
 def body(rhs, diag_inv, tiles, dest, obs_weight):
-    pattern = lax.all_gather(dest, "rows", axis=1, tiled=True)
+    pattern = jnp.concatenate(lax.all_gather(dest, "rows"), axis=1)
     current = rhs[0]
     solved_levels = []
     solved_block = current

time: 157 us -> 158 us (level)
  transfers between devices with their start and end apart: 3 -> 3, of which waited for: 2 -> 2; matrix products, arithmetic and copies ran while one was open for 0% -> 1% of each run, Pallas kernels for 0% -> 0%
where the time goes in v1:
time: 158 us; the launch traced here: 157 us
  blocking collectives  77.9 us (49%)
  waiting for transfers between devices  30.3 us (19%)
  matrix products  24.5 us (16%)
  starting transfers between devices  16.5 us (10%)
  local copies, waits for them, and re-layouts  5.68 us (4%)
    psum x1, blocking collectives, body(): observed = lax.psum(partial_sum, 'rows')  32 us
    all_gather x1, blocking collectives, body(): pattern = jnp.concatenate(lax.all_gather(dest, 'rows'), axis=1)  29.2 us
    all_to_all x2, waiting for transfers between devices, collect_updates(): lax.all_to_all(products, 'rows', split_axis=1, concat_axis=0, tiled=True)  18.3 us
    all_to_all x1, blocking collectives, collect_updates(): lax.all_to_all(partial_value, 'rows', split_axis=0, concat_axis=0, tiled=...  16.7 us
    dot_general x2, matrix products, collect_updates(): jnp.einsum('kab,bc->kac', tiles_level, solved_block, precision=lax.Precis...  12.3 us
    all_to_all x1, waiting for transfers between devices, collect_updates(): lax.all_to_all(partial_value, 'rows', split_axis=0, concat_axis=0, tiled=...  12 us
    all_to_all x2, starting transfers between devices, collect_updates(): lax.all_to_all(products, 'rows', split_axis=1, concat_axis=0, tiled=True)  11.2 us
    dot_general x3, matrix products, body(): jnp.dot(diag_inv[section], current, precision=lax.Precision.HIGHEST, pref...  11.1 us
  transfers between devices with their start and end apart: 3, of which 2 were waited for; matrix products, arithmetic and copies ran while one was open for 1% of the time, Pallas kernels for 0%

profile of v1, /device:TPU:0, one launch (start us, length us, event | category | flops | bytes accessed | tf_op | source)
XLA Modules:
  0.0 157.0 jit_solution(13151353748151247654)
XLA Ops:
  0.6 3.7 %fusion.10 = f32[768,128]{1,0:T(8,128)S(1)} fusion(f32[3,768,768]{2,1,0:T(8,128)} %param.6, f32[3,768,128]{2,1,0:T(8,128)} %param.5), kind=kOutput, calls=%fused_computation.10 | convolution fusion | flops 905969664 | bytes 3145728 | tf_op jit(solution)/shard_map/dot_general | solution.py:33
  4.3 7.4 %fusion.15 = f32[2,768,128]{1,2,0:T(8,128)S(1)} fusion(f32[2,2,768,768]{3,2,1,0:T(8,128)} %param.7, f32[768,128]{1,0:T(8,128)S(1)} %fusion.10), kind=kOutput, calls=%fused_computation.15 | convolution fusion | flops 1811939328 | bytes 5898240 | tf_op jit(solution)/shard_map/kab,bc->kac/dot_general | solution.py:8
  11.7 1.2 copy.30
  12.9 7.5 %all-to-all-start = ((f32[2,768,128]{2,0,1:T(2,128)}), f32[2,768,128]{2,0,1:T(2,128)S(1)}, u32[]{:S(2)}, u32[]{:S(2)}) async-start(f32[2,768,128]{2,0,1:T(2,128)} %copy.30), calls=%async_computation | async-start | bytes 1572864 | tf_op jit(solution)/shard_map/all_to_all | solution.py:18
  20.4 29.2 %all-gather = s32[32,1,2]{2,1,0:T(1,128)S(1)} all-gather(s32[2,1,2]{2,1,0:T(1,128)S(1)} %copy-done.3), channel_id=2, replica_groups=mesh['parts'=2,'rows'=16] {'rows'}, dimensions={0}, use_global_device_ids=true | all-gather | bytes 272 | tf_op jit(solution)/shard_map/all_gather | solution.py:28
  49.6 0.2 copy.43
  49.8 0.1 fusion.36
  49.9 0.2 copy.28
  50.1 0.1 eq.31
  50.2 0.1 copy.31
  50.3 0.6 copy.32
  50.9 0.4 fusion.29
  51.3 0.1 copy.33
  51.4 16.7 %all_to_all.46 = f32[16,48,128]{2,1,0:T(8,128)S(1)} all-to-all(f32[16,48,128]{2,1,0:T(8,128)S(1)} %copy.33), channel_id=1, replica_groups=mesh['parts'=2,'rows'=16] {'rows'}, dimensions={0} | all-to-all | bytes 786432 | tf_op jit(solution)/shard_map/all_to_all | solution.py:23
  68.1 0.1 bitcast_subtract_fusion.1
  68.2 3.8 %fusion.8 = f32[128,768]{1,0:T(8,128)S(1)} fusion(f32[3,768,768]{2,1,0:T(8,128)} %param.6, f32[1,768,128]{2,1,0:T(8,128)S(1)} %bitcast_subtract_fusion.1), kind=kOutput, calls=%fused_computation.8 | convolution fusion | flops 905969664 | bytes 3145728 | tf_op jit(solution)/shard_map/dot_general | solution.py:33
  72.0 5.0 %fusion.18 = f32[2,768,128]{1,2,0:T(8,128)S(1)} fusion(f32[2,2,768,768]{3,2,1,0:T(8,128)S(1)} %copy-done, f32[128,768]{1,0:T(8,128)S(1)} %fusion.8), kind=kOutput, calls=%fused_computation.16 | convolution fusion | flops 1811939328 | bytes 5898240 | tf_op jit(solution)/shard_map/kab,bc->kac/dot_general | solution.py:8
  76.9 1.2 copy.36
  78.1 3.6 %all-to-all-start.2 = ((f32[2,768,128]{2,0,1:T(2,128)}), f32[2,768,128]{2,0,1:T(2,128)S(1)}, u32[]{:S(2)}, u32[]{:S(2)}) async-start(f32[2,768,128]{2,0,1:T(2,128)} %copy.36), calls=%async_computation.2 | async-start | bytes 1572864 | tf_op jit(solution)/shard_map/all_to_all | solution.py:18
  81.7 0.2 copy.35
  81.9 0.1 eq.35
  82.0 18.3 %all-to-all-done.2 = f32[2,768,128]{2,0,1:T(2,128)S(1)} async-done(((f32[2,768,128]{2,0,1:T(2,128)}), f32[2,768,128]{2,0,1:T(2,128)S(1)}, u32[]{:S(2)}, u32[]{:S(2)}) %all-to-all-start.2) | async-done | bytes 786464 | tf_op jit(solution)/shard_map/all_to_all | solution.py:18
  100.4 0.6 copy.38
  101.1 0.4 fusion.32
  101.5 0.9 copy.39
  102.3 5.3 %all-to-all-start.3 = ((f32[16,48,128]{2,1,0:T(8,128)}), f32[16,48,128]{2,1,0:T(8,128)S(1)}, u32[]{:S(2)}, u32[]{:S(2)}) async-start(f32[16,48,128]{2,1,0:T(8,128)} %copy.39), calls=%async_computation.3 | async-start | bytes 786432 | tf_op jit(solution)/shard_map/all_to_all | solution.py:23
  107.7 0.2 copy.34
  107.8 12.0 %all-to-all-done.3 = f32[16,48,128]{2,1,0:T(8,128)S(1)} async-done(((f32[16,48,128]{2,1,0:T(8,128)}), f32[16,48,128]{2,1,0:T(8,128)S(1)}, u32[]{:S(2)}, u32[]{:S(2)}) %all-to-all-start.3) | async-done | bytes 393248 | tf_op jit(solution)/shard_map/all_to_all | solution.py:23
  119.9 3.7 %fusion.6 = f32[128,768]{0,1:T(8,128)S(1)} fusion(f32[3,768,768]{2,1,0:T(8,128)} %param.6, f32[1,768,128]{2,1,0:T(8,128)S(1)} %bitcast_subtract_fusion), kind=kOutput, calls=%fused_computation.6 | convolution fusion | flops 905969664 | bytes 3145728 | tf_op jit(solution)/shard_map/dot_general | solution.py:33
  123.5 0.3 convolution_bitcast_fusion
  123.8 32.0 %psum.7 = f32[128]{0:T(128)} all-reduce(f32[128]{0:T(128)S(1)} %convolution_bitcast_fusion), channel_id=1, replica_groups=mesh['parts'=2,'rows'=16] {'rows'}, use_global_device_ids=true, to_apply=%region_0.0 | all-reduce | flops 128 | bytes 1024 | tf_op jit(solution)/shard_map/psum | solution.py:50
  155.9 1.1 pad_maximum_fusion
  (12 shorter events, 0.1 us)
Async XLA Ops:
  11.7 8.7 %copy-start.3 = (s32[2,1,2]{2,1,0:T(1,128)S(1)}, s32[2,1,2]{2,1,0:T(1,128)}, u32[]{:S(2)}) copy-start(s32[2,1,2]{2,1,0:T(1,128)} %param.8) | copy-start | bytes 52
  12.9 55.2 %copy-start.1 = (f32[3,768,128]{2,1,0:T(8,128)S(1)}, f32[3,768,128]{2,1,0:T(8,128)}, u32[]{:S(2)}) copy-start(f32[3,768,128]{2,1,0:T(8,128)} %param.5) | copy-start | bytes 3538948
  12.9 37.3 %all-to-all-start = ((f32[2,768,128]{2,0,1:T(2,128)}), f32[2,768,128]{2,0,1:T(2,128)S(1)}, u32[]{:S(2)}, u32[]{:S(2)}) async-start(f32[2,768,128]{2,0,1:T(2,128)} %copy.30), calls=%async_computation | async-start | bytes 1572864 | tf_op jit(solution)/shard_map/all_to_all | solution.py:18
  50.2 21.7 %copy-start = (f32[2,2,768,768]{3,2,1,0:T(8,128)S(1)}, f32[2,2,768,768]{3,2,1,0:T(8,128)}, u32[]{:S(2)}) copy-start(f32[2,2,768,768]{3,2,1,0:T(8,128)} %param.7) | copy-start | bytes 28311556
  78.1 22.3 %all-to-all-start.2 = ((f32[2,768,128]{2,0,1:T(2,128)}), f32[2,768,128]{2,0,1:T(2,128)S(1)}, u32[]{:S(2)}, u32[]{:S(2)}) async-start(f32[2,768,128]{2,0,1:T(2,128)} %copy.36), calls=%async_computation.2 | async-start | bytes 1572864 | tf_op jit(solution)/shard_map/all_to_all | solution.py:18
  100.4 7.2 %copy-start.2 = (f32[768]{0:T(1024)S(1)}, f32[768]{0:T(1024)}, u32[]{:S(2)}) copy-start(f32[768]{0:T(1024)} %param.9) | copy-start | bytes 9220
  102.3 17.5 %all-to-all-start.3 = ((f32[16,48,128]{2,1,0:T(8,128)}), f32[16,48,128]{2,1,0:T(8,128)S(1)}, u32[]{:S(2)}, u32[]{:S(2)}) async-start(f32[16,48,128]{2,1,0:T(8,128)} %copy.39), calls=%async_computation.3 | async-start | bytes 786432 | tf_op jit(solution)/shard_map/all_to_all | solution.py:23
